TPU v7x, 512 devices: a whole 4x8x8 slice. The times are simulated.
512 devices in a mesh: item: 16 (over y, core), user: 32 (over z, x).
Axes of the slice: x: 4, y: 8, z: 8, core: 2. Of those that a mesh axis runs over, the one named last changes fastest.
Arguments:
- item_factors: float32 [32768, 128], P('item')
- tile_lists: int32 [512, 16], P(('item', 'user')), may hold values from 0 to 255, as said below
- tile_weights: bfloat16 [512, 16, 128, 128], P(('item', 'user')), may hold values from 0 to 40
- user_factors: float32 [65536, 128], P(('item', 'user')), may hold values from -6 to 6
Outputs:
- new_factors: float32 [65536, 128], P(('item', 'user'))
Inputs may be any that keep to these rules, and one draw needn't show every extreme that they name: `tile_lists`: item shard s holds tiles s * 16 to (s + 1) * 16 - 1. Among the 16 slots of one device's blocks, at most 2 name tiles of one item shard, and for some shard exactly 2 do; a tile may be named more than once.
All inputs are finite; a program needn't handle non-finite values.
Results may differ from a plain program's by a relative error of at most 0.0024.
Values sent between devices are 32-bit elements; how exact they have to be, the bound alone decides.
No kernel may reach another device: no remote copies, remote signals or barrier semaphores. Data moves between devices by JAX's collectives and lax.ppermute only.
A program may use at most 64 MiB of HBM per device.

v0:
```python
import jax
import jax.numpy as jnp
from jax import lax
from jax.sharding import PartitionSpec as P

ITERS = 4
RIDGE_WEIGHT = 0.1
EPSILON = 1e-06
HIGHEST = lax.Precision.HIGHEST


def apply_system(vectors, tiles, weights, gram):
    scores = jnp.einsum("bur,bkir->bkui", vectors, tiles, precision=HIGHEST)
    spread = jnp.einsum("bkui,bkir->bur", scores * weights, tiles, precision=HIGHEST)
    return (
        spread
        + jnp.einsum("bur,rs->bus", vectors, gram, precision=HIGHEST)
        + RIDGE_WEIGHT * vectors
    )


def conjugate(start, tiles, weights, gram, steps):
    weights = weights.astype(jnp.float32)
    target = jnp.einsum("bkui,bkir->bur", 1.0 + weights, tiles, precision=HIGHEST)
    answer = start
    resid = target - apply_system(start, tiles, weights, gram)
    direction = resid
    norm_now = jnp.sum(resid * resid, axis=-1, keepdims=True)
    for step_index in range(steps):
        image = apply_system(direction, tiles, weights, gram)
        alpha = norm_now / (jnp.sum(direction * image, axis=-1, keepdims=True) + EPSILON)
        answer = answer + alpha * direction
        resid = resid - alpha * image
        norm_next = jnp.sum(resid * resid, axis=-1, keepdims=True)
        direction = resid + norm_next / (norm_now + EPSILON) * direction
        norm_now = norm_next
    return answer


def local(item_factors, tile_lists, tile_weights, user_factors):
    factor_rank = item_factors.shape[1]
    tile_side = tile_weights.shape[-1]
    blocks_here, slots_here = tile_lists.shape
    shard_rows = item_factors.shape[0]
    user_parts = lax.axis_size("user")
    share_rows = shard_rows // user_parts
    piece = lax.dynamic_slice_in_dim(
        item_factors, lax.axis_index("user") * share_rows, share_rows, 0
    )
    partial_gram = jnp.dot(piece.T, piece, precision=HIGHEST, preferred_element_type=jnp.float32)
    gram = lax.psum(partial_gram, ("item", "user"))
    tile_ids = tile_lists.reshape(-1)
    all_rows = lax.all_gather(item_factors, "item", axis=0, tiled=True)
    fetched = all_rows.reshape(-1, tile_side, factor_rank)[tile_ids]
    tiles = fetched.reshape(blocks_here, slots_here, tile_side, factor_rank)
    start = user_factors.reshape(blocks_here, tile_side, factor_rank)
    solved = conjugate(start, tiles, tile_weights, gram, ITERS)
    return solved.reshape(-1, factor_rank)


def solution(mesh):
    in_specs = (
        P("item", None),
        P(("item", "user"), None),
        P(("item", "user"), None, None, None),
        P(("item", "user"), None),
    )
    out_specs = P(("item", "user"), None)
    return jax.shard_map(local, mesh=mesh, in_specs=in_specs, out_specs=out_specs, check_vma=False)
```

profile of v0, /device:TPU:1, one launch (start us, length us, event | category | flops | bytes accessed | tf_op | source)
XLA Modules:
  0.0 362.3 jit_solution(888267724627594206)
XLA Ops:
  7.4 0.0 all-gather.2.cloned.1.call-start
  7.4 0.7 all-gather.2.cloned.1.call-update
  8.1 0.0 all-reduce.2.cloned.1.call-start
  8.1 1.8 fusion.22
  9.9 0.0 all-reduce.2.cloned.1.call-update
  9.9 0.7 fusion.24
  10.6 1.3 copy.24
  11.9 0.9 copy.33
  12.8 101.3 %all-gather.2.cloned.1.call-done = f32[32768,128]{1,0:T(8,128)} async-done(((f32[2048,128]{1,0:T(8,128)}), f32[32768,128]{1,0:T(8,128)}) %all-gather.2.cloned.1.call-update) | async-done | bytes 16777232 | tf_op jit(solution)/shard_map/all_gather | solution.py:53
  114.2 6.4 %gather_fusion = f32[16,128,128]{2,1,0:T(8,128)S(1)} fusion(f32[256,128,128]{2,1,0:T(8,128)} %bitcast.119, s32[1024]{0:T(1024)S(1)} %pad_clamp_fusion), kind=kCustom, calls=%fused_computation | custom fusion | bytes 2097216 | tf_op jit(solution)/shard_map/gather | solution.py:54
  120.6 1.8 fusion
  122.4 1.8 convolution_bitcast_fusion.10
  124.2 1.8 convolution_bitcast_fusion.11
  126.1 211.4 %all-reduce.2.cloned.1.call-done = f32[128,128]{1,0:T(8,128)} async-done(((f32[128,128]{1,0:T(8,128)}), f32[128,128]{1,0:T(8,128)}) %all-reduce.2.cloned.1.call-update) | async-done | bytes 65552 | tf_op jit(solution)/shard_map/psum | solution.py:51
  337.5 0.0 copy-start
  337.5 1.2 fusion.12
  338.7 1.0 fusion.1
  339.7 1.8 convolution_bitcast_fusion.8
  341.5 1.1 multiply_reduce_fusion.5
  342.7 1.0 fusion.2
  343.7 1.8 convolution_bitcast_fusion.7
  345.5 1.1 multiply_reduce_fusion.3
  346.8 1.2 fusion.3
  347.9 1.8 convolution_bitcast_fusion.6
  349.8 1.1 multiply_reduce_fusion.1
  351.0 1.0 fusion.4
  352.0 1.8 convolution_bitcast_fusion.5
  353.8 0.0 copy-done
  353.8 0.3 fusion.13
  354.2 0.7 copy.43
  (15 shorter events, 0.3 us)
Async XLA Ops:
  7.4 106.8 %all-gather.2.cloned.1.call-start = ((), (), s32[]{:S(2)}) async-start(), calls=%async_computation | async-start | bytes 17825792 | tf_op jit(solution)/shard_map/all_gather | solution.py:53
  8.1 329.4 %all-reduce.2.cloned.1.call-start = ((), (), s32[]{:S(2)}) async-start(), calls=%async_computation.1 | async-start | bytes 131072 | tf_op jit(solution)/shard_map/psum | solution.py:51
  337.5 16.3 %copy-start = (f32[128,128]{1,0:T(8,128)S(1)}, f32[128,128]{1,0:T(8,128)}, u32[]{:S(2)}) copy-start(f32[128,128]{1,0:T(8,128)} %all-reduce.2.cloned.1.call-done) | copy-start | bytes 196612
Sparse Core Ops, SparseCore 0:
  10.3 103.8 all-gather.1
Sparse Core Ops, SparseCore 1:
  13.6 323.9 all-reduce.1
where the time goes:
time: 363 us; the launch traced here: 362 us
  waiting for transfers between devices  313 us (86%)
  matrix products  23.5 us (6%)
  between operations  15 us (4%)
  local copies, waits for them, and re-layouts  9.38 us (3%)
    psum x1, waiting for transfers between devices, local(): gram = lax.psum(partial_gram, ('item', 'user'))  211 us
    all_gather x1, waiting for transfers between devices, local(): all_rows = lax.all_gather(item_factors, 'item', axis=0, tiled=True)  101 us
    dot_general x5, matrix products, apply_system(): jnp.einsum('bkui,bkir->bur', scores * weights, tiles, precision=HIGHEST)  9.1 us
  transfers between devices with their start and end apart: 2, of which 2 were waited for; matrix products, arithmetic and copies ran while one was open for 5% of the time, Pallas kernels for 0%

commit v1 on v0

--- a/solution.py
+++ b/solution.py
@@ -48,7 +48,7 @@
         item_factors, lax.axis_index("user") * share_rows, share_rows, 0
     )
     partial_gram = jnp.dot(piece.T, piece, precision=HIGHEST, preferred_element_type=jnp.float32)
-    gram = lax.psum(partial_gram, ("item", "user"))
+    gram = lax.psum(lax.psum(partial_gram, "item"), "user")
     tile_ids = tile_lists.reshape(-1)
     all_rows = lax.all_gather(item_factors, "item", axis=0, tiled=True)
     fetched = all_rows.reshape(-1, tile_side, factor_rank)[tile_ids]

time: 363 us -> 399 us (1.099)
  waiting for transfers between devices: 313 us -> 348 us
    psum x1 -> x2, waiting for transfers between devices: 211 us -> 248 us  [local(): gram = lax.psum(lax.psum(partial_gram, 'item'), 'user')]
  transfers between devices with their start and end apart: 2 -> 3, of which waited for: 2 -> 3; matrix products, arithmetic and copies ran while one was open for 5% -> 4% of each run, Pallas kernels for 0% -> 0%
where the time goes in v1:
time: 399 us; the launch traced here: 395 us
  waiting for transfers between devices  348 us (87%)
  matrix products  23.5 us (6%)
  between operations  13.2 us (3%)
  local copies, waits for them, and re-layouts  9.36 us (2%)
    psum x2, waiting for transfers between devices, local(): gram = lax.psum(lax.psum(partial_gram, 'item'), 'user')  248 us
    all_gather x1, waiting for transfers between devices, local(): all_rows = lax.all_gather(item_factors, 'item', axis=0, tiled=True)  98.7 us
    dot_general x5, matrix products, apply_system(): jnp.einsum('bkui,bkir->bur', scores * weights, tiles, precision=HIGHEST)  9.1 us
  transfers between devices with their start and end apart: 3, of which 3 were waited for; matrix products, arithmetic and copies ran while one was open for 4% of the time, Pallas kernels for 0%

profile of v1, /device:TPU:1, one launch (start us, length us, event | category | flops | bytes accessed | tf_op | source)
XLA Modules:
  0.0 395.1 jit_solution(348700483169526037)
XLA Ops:
  6.5 0.0 all-reduce.3.cloned.1.call-start
  6.5 1.8 fusion.22
  8.3 0.0 all-reduce.3.cloned.1.call-update
  8.3 0.0 all-gather.2.cloned.1.call-start
  8.4 0.7 all-gather.2.cloned.1.call-update
  9.1 0.0 all-reduce.5.cloned.1.call-start
  9.1 1.3 copy.24
  10.4 0.9 copy.33
  11.4 0.7 fusion.24
  12.0 109.6 %all-reduce.3.cloned.1.call-done = f32[128,128]{1,0:T(8,128)} async-done(((f32[128,128]{1,0:T(8,128)}), f32[128,128]{1,0:T(8,128)}) %all-reduce.3.cloned.1.call-update) | async-done | bytes 65552 | tf_op jit(solution)/shard_map/psum | solution.py:51
  121.6 0.0 all-reduce.5.cloned.1.call-update
  121.6 98.7 %all-gather.2.cloned.1.call-done = f32[32768,128]{1,0:T(8,128)} async-done(((f32[2048,128]{1,0:T(8,128)}), f32[32768,128]{1,0:T(8,128)}) %all-gather.2.cloned.1.call-update) | async-done | bytes 16777232 | tf_op jit(solution)/shard_map/all_gather | solution.py:53
  220.4 6.4 %gather_fusion = f32[16,128,128]{2,1,0:T(8,128)S(1)} fusion(f32[256,128,128]{2,1,0:T(8,128)} %bitcast.119, s32[1024]{0:T(1024)S(1)} %pad_clamp_fusion), kind=kCustom, calls=%fused_computation | custom fusion | bytes 2097216 | tf_op jit(solution)/shard_map/gather | solution.py:54
  226.8 1.8 fusion
  228.6 1.8 convolution_bitcast_fusion.10
  230.4 1.8 convolution_bitcast_fusion.11
  232.2 138.9 %all-reduce.5.cloned.1.call-done = f32[128,128]{1,0:T(8,128)} async-done(((f32[128,128]{1,0:T(8,128)}), f32[128,128]{1,0:T(8,128)}) %all-reduce.5.cloned.1.call-update) | async-done | bytes 65552 | tf_op jit(solution)/shard_map/psum | solution.py:51
  371.1 0.0 copy-start
  371.1 1.2 fusion.12
  372.3 1.0 fusion.1
  373.3 1.8 convolution_bitcast_fusion.8
  375.1 1.1 multiply_reduce_fusion.5
  376.4 1.0 fusion.2
  377.3 1.8 convolution_bitcast_fusion.7
  379.1 1.1 multiply_reduce_fusion.3
  380.4 1.2 fusion.3
  381.6 1.8 convolution_bitcast_fusion.6
  383.4 1.1 multiply_reduce_fusion.1
  384.6 1.0 fusion.4
  385.6 1.8 convolution_bitcast_fusion.5
  387.4 0.0 copy-done
  387.4 0.3 fusion.13
  387.8 0.7 copy.43
  (15 shorter events, 0.3 us)
Async XLA Ops:
  6.5 115.1 %all-reduce.3.cloned.1.call-start = ((), (), s32[]{:S(2)}) async-start(), calls=%async_computation.1 | async-start | bytes 131072 | tf_op jit(solution)/shard_map/psum | solution.py:51
  8.3 212.1 %all-gather.2.cloned.1.call-start = ((), (), s32[]{:S(2)}) async-start(), calls=%async_computation | async-start | bytes 17825792 | tf_op jit(solution)/shard_map/all_gather | solution.py:53
  9.1 362.0 %all-reduce.5.cloned.1.call-start = ((), (), s32[]{:S(2)}) async-start(), calls=%async_computation.2 | async-start | bytes 131072 | tf_op jit(solution)/shard_map/psum | solution.py:51
  371.1 16.3 %copy-start = (f32[128,128]{1,0:T(8,128)S(1)}, f32[128,128]{1,0:T(8,128)}, u32[]{:S(2)}) copy-start(f32[128,128]{1,0:T(8,128)} %all-reduce.5.cloned.1.call-done) | copy-start | bytes 196612
Sparse Core Ops, SparseCore 0:
  9.7 111.9 all-reduce.2
  123.7 96.6 all-gather.1
  223.8 147.2 all-reduce.4
